TPU v7x, 128 devices: a whole 4x4x4 slice. The times are simulated.
128 devices in a mesh: row: 8 (over z, core), col: 16 (over y, x).
Axes of the slice: x: 4, y: 4, z: 4, core: 2. Of those that a mesh axis runs over, the one named last changes fastest.
Arguments:
- right_side: float32 [8, 65536], P(None, ('row', 'col')), may hold values from -30 to 30
- u_factors: bfloat16 [128, 128, 48, 512], P(('row', 'col')), may hold values from -0.078125 to 0.078125
- v_factors: bfloat16 [128, 128, 48, 512], P('row', 'col'), may hold values from -0.25 to 0.25
- ranks: int32 [128, 128], P('row', 'col'), may hold values from 8 to 48
- far_blocks: bfloat16 [16, 512, 65536], P('row', None, 'col'), may hold values from -0.09375 to 0.09375
- block_target: int32 [16, 16], replicated, may hold values from 0 to 127, as said below
- recv_order: int32 [128], replicated, may hold values from 0 to 127, as said below
Outputs:
- densities: float32 [8, 65536], P(None, 'col')
- residual: float32 [8, 65536], P(None, ('row', 'col'))
- far_field: float32 [128, 4096], P(('row', 'col'))
Inputs may be any that keep to these rules, and one draw needn't show every extreme that they name: `recv_order`: a permutation of the receiver patches. `block_target`: block (b, c) with b % 2 == 0 lies on device g = (b // 2) * 16 + c; its receiver patch is stored in output rows owned by device (g + 128 / 2) mod 128 if g is even and by device g - 1 if g is odd; the other blocks may name any receiver patch.
All inputs are finite; a program needn't handle non-finite values.
Results may differ from a plain program's by a relative error of at most 0.008.
Values may be sent and summed in bfloat16 or wider, within the bound.
No kernel may reach another device: no remote copies, remote signals or barrier semaphores. Data moves between devices by JAX's collectives and lax.ppermute only.
A program may use at most 128 MiB of HBM per device.

v0:
```python
import jax
import jax.numpy as jnp
from jax import lax
from jax.sharding import PartitionSpec as P

ITERS = 2


def per_device(right_side, u_factors, v_factors, ranks, far_blocks, block_target, recv_order):
    dens_count = right_side.shape[0]
    own_rows = u_factors.shape[0]
    all_cols = u_factors.shape[1]
    slot_count = u_factors.shape[2]
    patch_len = u_factors.shape[3]
    group_rows = v_factors.shape[0]
    own_cols = v_factors.shape[1]
    slot_index = lax.broadcasted_iota(jnp.int32, (group_rows, own_cols, slot_count, 1), 2)
    kept = (slot_index < ranks[:, :, None, None]).astype(jnp.float32)
    kept_half = kept.astype(jnp.bfloat16)
    residual = right_side
    densities = jnp.zeros((dens_count, own_cols * patch_len), jnp.float32)
    for iteration in range(ITERS):
        res_bf = residual.astype(jnp.bfloat16).reshape(dens_count, own_rows, patch_len)
        back_coef = jnp.einsum(
            "ijsp,dip->ijsd", u_factors, res_bf, preferred_element_type=jnp.float32
        )
        back_coef = back_coef.astype(jnp.bfloat16).reshape(
            own_rows, all_cols, slot_count * dens_count
        )
        arrived = lax.all_to_all(back_coef, "col", split_axis=1, concat_axis=0, tiled=True)
        arrived = arrived.reshape(group_rows, own_cols, slot_count, dens_count) * kept_half
        partial_grad = jnp.einsum(
            "ijsp,ijsd->djp", v_factors, arrived, preferred_element_type=jnp.float32
        )
        grad = lax.psum(partial_grad.reshape(dens_count, own_cols * patch_len), "row")
        grad_local = jnp.sum(grad * grad, axis=1)
        grad_sq = lax.psum(grad_local, "col")
        grad_bf = grad.astype(jnp.bfloat16).reshape(dens_count, own_cols, patch_len)
        coefficients = (
            jnp.einsum("ijsp,djp->ijsd", v_factors, grad_bf, preferred_element_type=jnp.float32)
            * kept
        )
        coefficients = coefficients.astype(jnp.bfloat16).reshape(
            group_rows, own_cols, slot_count * dens_count
        )
        landed = lax.all_to_all(coefficients, "col", split_axis=0, concat_axis=1, tiled=True)
        landed = landed.reshape(own_rows, all_cols, slot_count, dens_count)
        image = jnp.einsum("ijsp,ijsd->dip", u_factors, landed, preferred_element_type=jnp.float32)
        image = image.reshape(dens_count, own_rows * patch_len)
        image_local = jnp.sum(image * image, axis=1)
        image_sq = lax.psum(image_local, ("row", "col"))
        step_size = grad_sq / (image_sq + 1e-06)
        densities = densities + step_size[:, None] * grad
        residual = residual - step_size[:, None] * image
    block_count = far_blocks.shape[0]
    x_half = densities.astype(jnp.bfloat16)
    block_field = jnp.einsum("bpn,dn->bdp", far_blocks, x_half, preferred_element_type=jnp.float32)
    block_field = block_field.reshape(block_count, dens_count * patch_len)
    local_target = lax.dynamic_slice(
        block_target, (lax.axis_index("row") * block_count, lax.axis_index("col")), (block_count, 1)
    ).reshape(block_count)
    onehot = (local_target[:, None] == recv_order[None, :]).astype(jnp.float32)
    far_field = lax.psum_scatter(
        jnp.dot(
            onehot.T,
            block_field,
            preferred_element_type=jnp.float32,
            precision=lax.Precision.HIGHEST,
        ),
        ("row", "col"),
        scatter_dimension=0,
        tiled=True,
    )
    return (densities, residual, far_field)


def solution(mesh):
    return jax.shard_map(
        per_device,
        mesh=mesh,
        in_specs=(
            P(None, ("row", "col")),
            P(("row", "col"), None, None, None),
            P("row", "col", None, None),
            P("row", "col"),
            P("row", None, "col"),
            P(),
            P(),
        ),
        out_specs=(P(None, "col"), P(None, ("row", "col")), P(("row", "col"), None)),
        check_vma=False,
    )
```

profile of v0, /device:TPU:1, one launch (start us, length us, event | category | flops | bytes accessed | tf_op | source)
XLA Modules:
  0.0 595.4 jit_solution(9957855549774173676)
XLA Ops:
  7.2 0.0 copy-start
  7.2 0.0 copy-start.5
  7.2 5.9 convolution_convert_fusion
  13.1 0.2 copy.50
  13.3 0.2 copy.51
  13.5 0.5 broadcast.22
  14.0 1.2 reduce.6
  15.2 0.7 reshape.129
  15.9 7.6 %all-to-all-start = ((bf16[16,2,1536]{2,1,0:T(2,128)(2,1)}), bf16[16,2,1536]{2,1,0:T(2,128)(2,1)S(1)}, u32[]{:S(2)}, u32[]{:S(2)}) async-start(bf16[16,2,1536]{2,1,0:T(2,128)(2,1)} %reshape.129), calls=%async_computation | async-start | bytes 196608 | tf_op jit(solution)/shard_map/all_to_all | solution.py:30
  23.5 0.0 all-reduce.5.cloned.1.call-start
  23.5 0.0 copy-done.5
  23.6 0.1 fusion.38
  23.7 6.6 %all-to-all-done = bf16[16,2,1536]{2,1,0:T(2,128)(2,1)S(1)} async-done(((bf16[16,2,1536]{2,1,0:T(2,128)(2,1)}), bf16[16,2,1536]{2,1,0:T(2,128)(2,1)S(1)}, u32[]{:S(2)}, u32[]{:S(2)}) %all-to-all-start) | async-done | bytes 98336 | tf_op jit(solution)/shard_map/all_to_all | solution.py:30
  30.2 0.1 reshape.130
  30.3 0.6 bitcast_reduce_fusion.1
  30.9 1.8 reshape.105
  32.6 4.8 fusion.8
  37.4 0.0 all-reduce.5.cloned.1.call-update
  37.4 58.2 %all-reduce.5.cloned.1.call-done = f32[8,4096]{1,0:T(8,128)} async-done(((f32[8,4096]{1,0:T(8,128)}), f32[8,4096]{1,0:T(8,128)}) %all-reduce.5.cloned.1.call-update) | async-done | bytes 131088 | tf_op jit(solution)/shard_map/psum | solution.py:35
  95.6 1.1 multiply_reduce_fusion.1
  96.7 5.9 fusion.22
  102.6 0.5 copy.55
  103.1 0.9 copy.56
  104.1 6.5 %all-to-all-start.1 = ((bf16[16,8,384]{2,1,0:T(8,128)(2,1)}), bf16[16,8,384]{2,1,0:T(8,128)(2,1)S(1)}, u32[]{:S(2)}, u32[]{:S(2)}) async-start(bf16[16,8,384]{2,1,0:T(8,128)(2,1)} %copy.56), calls=%async_computation.1 | async-start | bytes 196608 | tf_op jit(solution)/shard_map/all_to_all | solution.py:46
  110.6 0.0 all-reduce.7.cloned.1.call-start
  110.6 33.3 %psum.43 = f32[8]{0:T(128)S(1)} all-reduce(f32[8]{0:T(128)S(1)} %get-tuple-element.5), channel_id=1, replica_groups=mesh['row'=8,'col'=16] {'col'}, use_global_device_ids=true, to_apply=%region_2.0 | all-reduce | flops 8 | bytes 64 | tf_op jit(solution)/shard_map/psum | solution.py:37
  144.0 0.0 all-to-all-done.1
  144.0 1.8 reshape.109
  145.8 3.8 multiply_reduce_fusion.3
  149.6 72.1 %psum.44 = f32[8]{0:T(128)S(1)} all-reduce(f32[8]{0:T(128)S(1)} %get-tuple-element.9), channel_id=1, replica_groups=mesh['row'=8,'col'=16] {'row','col'}, use_global_device_ids=true, to_apply=%region_4.0 | all-reduce | flops 8 | bytes 64 | tf_op jit(solution)/shard_map/psum | solution.py:51
  221.7 0.0 copy-done.4
  221.7 9.4 %fusion.31 = bf16[1,128,384]{1,2,0:T(8,128)(2,1)S(1)} fusion(bf16[128,48,512]{2,1,0:T(8,128)(2,1)} %bitcast.81, f32[8,512]{1,0:T(8,128)S(1)} %copy-done.4, f32[8,512]{1,0:T(8,128)S(1)} %get-tuple-element.10, f32[8]{0:T(128)S(1)} %add_divide_fusion.1), kind=kOutput, calls=%fused_computation.18 | convolution fusion | flops 50393088 | bytes 6422560 | tf_op jit(solution)/shard_map/ijsp,dip->ijsd/dot_general | solution.py:24
  231.1 0.2 copy.59
  231.3 1.2 reduce.7
  232.6 10.2 %all_to_all.16 = bf16[16,2,1536]{2,1,0:T(2,128)(2,1)S(1)} all-to-all(bf16[16,2,1536]{2,1,0:T(2,128)(2,1)S(1)} %reshape.131), channel_id=1, replica_groups=mesh['row'=8,'col'=16] {'col'}, dimensions={0} | all-to-all | bytes 196608 | tf_op jit(solution)/shard_map/all_to_all | solution.py:30
  242.8 0.1 reshape.132
  242.9 0.6 bitcast_reduce_fusion
  243.5 1.8 reshape.111
  245.2 4.8 fusion.6
  250.0 0.0 all-reduce.7.cloned.1.call-update
  250.1 55.2 %all-reduce.7.cloned.1.call-done = f32[8,4096]{1,0:T(8,128)} async-done(((f32[8,4096]{1,0:T(8,128)}), f32[8,4096]{1,0:T(8,128)}) %all-reduce.7.cloned.1.call-update) | async-done | bytes 131088 | tf_op jit(solution)/shard_map/psum | solution.py:35
  305.3 1.1 fusion.51
  306.4 5.9 fusion.25
  312.3 0.5 copy.62
  312.8 0.9 copy.63
  313.7 6.5 %all-to-all-start.3 = ((bf16[16,8,384]{2,1,0:T(8,128)(2,1)}), bf16[16,8,384]{2,1,0:T(8,128)(2,1)S(1)}, u32[]{:S(2)}, u32[]{:S(2)}) async-start(bf16[16,8,384]{2,1,0:T(8,128)(2,1)} %copy.63), calls=%async_computation.3 | async-start | bytes 196608 | tf_op jit(solution)/shard_map/all_to_all | solution.py:46
  320.3 0.0 all-reduce.9.cloned.1.call-start
  320.3 0.0 copy-done
  320.3 0.2 dynamic-slice_reduce_fusion
  320.5 33.2 %psum.46 = f32[8]{0:T(128)S(1)} all-reduce(f32[8]{0:T(128)S(1)} %get-tuple-element.4), channel_id=1, replica_groups=mesh['row'=8,'col'=16] {'col'}, use_global_device_ids=true, to_apply=%region_7.0 | all-reduce | flops 8 | bytes 64 | tf_op jit(solution)/shard_map/psum | solution.py:37
  353.8 0.0 all-to-all-done.3
  353.8 1.8 reshape.115
  355.5 3.8 multiply_reduce_fusion.2
  359.4 0.0 copy-start.6
  359.4 72.0 %psum.47 = f32[8]{0:T(128)S(1)} all-reduce(f32[8]{0:T(128)S(1)} %get-tuple-element.11), channel_id=1, replica_groups=mesh['row'=8,'col'=16] {'row','col'}, use_global_device_ids=true, to_apply=%region_9.0 | all-reduce | flops 8 | bytes 64 | tf_op jit(solution)/shard_map/psum | solution.py:51
  431.4 0.0 copy-done.2
  431.4 0.1 multiply_add_fusion
  431.5 0.0 copy-start.1
  431.5 5.7 convolution_bitcast_fusion
  437.3 2.4 fusion.44
  439.7 0.0 all-reduce.9.cloned.1.call-update
  439.7 0.7 multiply_subtract_fusion
  440.4 146.9 %all-reduce.9.cloned.1.call-done = f32[128,4096]{1,0:T(8,128)} async-done(((f32[128,4096]{1,0:T(8,128)}), f32[128,4096]{1,0:T(8,128)}) %all-reduce.9.cloned.1.call-update) | async-done | bytes 2097168
  587.3 1.5 constant_dynamic-slice_fusion
  (11 shorter events, 0.1 us)
Async XLA Ops:
  7.2 313.2 %copy-start = (s32[16,16]{1,0:T(8,128)S(1)}, s32[16,16]{1,0:T(8,128)}, u32[]{:S(2)}) copy-start(s32[16,16]{1,0:T(8,128)} %param.12) | copy-start | bytes 3076
  7.2 16.4 %copy-start.5 = (s32[16,8]{0,1:T(8,128)S(1)}, s32[16,8]{0,1:T(8,128)}, u32[]{:S(2)}) copy-start(s32[16,8]{0,1:T(8,128)} %param.10) | copy-start | bytes 1540
  15.9 14.3 %all-to-all-start = ((bf16[16,2,1536]{2,1,0:T(2,128)(2,1)}), bf16[16,2,1536]{2,1,0:T(2,128)(2,1)S(1)}, u32[]{:S(2)}, u32[]{:S(2)}) async-start(bf16[16,2,1536]{2,1,0:T(2,128)(2,1)} %reshape.129), calls=%async_computation | async-start | bytes 196608 | tf_op jit(solution)/shard_map/all_to_all | solution.py:30
  23.5 72.1 %all-reduce.5.cloned.1.call-start = ((), (), s32[]{:S(2)}) async-start(), calls=%async_computation.4 | async-start | bytes 262144 | tf_op jit(solution)/shard_map/psum | solution.py:35
  102.6 119.1 %copy-start.4 = (f32[8,512]{1,0:T(8,128)S(1)}, f32[8,512]{1,0:T(8,128)}, u32[]{:S(2)}) copy-start(f32[8,512]{1,0:T(8,128)} %param.7) | copy-start | bytes 49156
  104.1 39.9 %all-to-all-start.1 = ((bf16[16,8,384]{2,1,0:T(8,128)(2,1)}), bf16[16,8,384]{2,1,0:T(8,128)(2,1)S(1)}, u32[]{:S(2)}, u32[]{:S(2)}) async-start(bf16[16,8,384]{2,1,0:T(8,128)(2,1)} %copy.56), calls=%async_computation.1 | async-start | bytes 196608 | tf_op jit(solution)/shard_map/all_to_all | solution.py:46
  110.6 194.7 %all-reduce.7.cloned.1.call-start = ((), (), s32[]{:S(2)}) async-start(), calls=%async_computation.5 | async-start | bytes 262144 | tf_op jit(solution)/shard_map/psum | solution.py:35
  312.3 119.2 %copy-start.2 = (f32[8,4096]{1,0:T(8,128)S(1)}, f32[8,4096]{1,0:T(8,128)}, u32[]{:S(2)}) copy-start(f32[8,4096]{1,0:T(8,128)} %all-reduce.5.cloned.1.call-done) | copy-start | bytes 393220
  312.3 119.2 %copy-start.3 = (f32[8,4096]{1,0:T(8,128)S(1)}, f32[8,4096]{1,0:T(8,128)}, u32[]{:S(2)}) copy-start(f32[8,4096]{1,0:T(8,128)} %all-reduce.7.cloned.1.call-done) | copy-start | bytes 393220
  313.7 40.0 %all-to-all-start.3 = ((bf16[16,8,384]{2,1,0:T(8,128)(2,1)}), bf16[16,8,384]{2,1,0:T(8,128)(2,1)S(1)}, u32[]{:S(2)}, u32[]{:S(2)}) async-start(bf16[16,8,384]{2,1,0:T(8,128)(2,1)} %copy.63), calls=%async_computation.3 | async-start | bytes 196608 | tf_op jit(solution)/shard_map/all_to_all | solution.py:46
  320.3 267.1 %all-reduce.9.cloned.1.call-start = ((), (), s32[]{:S(2)}) async-start(), calls=%async_computation.6 | async-start | bytes 4194304
  359.4 77.9 %copy-start.6 = (s32[128]{0:T(128)S(1)}, s32[128]{0:T(128)}, u32[]{:S(2)}) copy-start(s32[128]{0:T(128)} %param.13) | copy-start | bytes 1540
  431.5 8.2 %copy-start.1 = (f32[8,4096]{1,0:T(8,128)}, f32[8,4096]{1,0:T(8,128)S(1)}, u32[]{:S(2)}) copy-start(f32[8,4096]{1,0:T(8,128)S(1)} %multiply_add_fusion) | copy-start | bytes 393220
Sparse Core Ops, SparseCore 0:
  37.6 58.0 all-reduce.4
  250.2 55.0 all-reduce.6
  439.8 147.4 all-reduce.8
where the time goes:
time: 596 us; the launch traced here: 595 us
  waiting for transfers between devices  267 us (45%)
  blocking collectives  221 us (37%)
  matrix products  52.3 us (9%)
  starting transfers between devices  20.8 us (3%)
  local copies, waits for them, and re-layouts  15 us (3%)
  between operations  14 us (2%)
    unnamed x4, waiting for transfers between devices  147 us
    psum x2, blocking collectives, per_device(): image_sq = lax.psum(image_local, ('row', 'col'))  144 us
    psum x2, waiting for transfers between devices, per_device(): lax.psum(partial_grad.reshape(dens_count, own_cols * patch_len), 'row')  113 us
    psum x2, blocking collectives, per_device(): grad_sq = lax.psum(grad_local, 'col')  66.6 us
    dot_general x2, matrix products, per_device(): jnp.einsum('ijsp,dip->ijsd', u_factors, res_bf, preferred_element_type=jn...  15.3 us
    all_to_all x2, starting transfers between devices, per_device(): lax.all_to_all(coefficients, 'col', split_axis=0, concat_axis=1, tiled=True)  13.1 us
  transfers between devices with their start and end apart: 6, of which 4 were waited for; matrix products, arithmetic and copies ran while one was open for 0% of the time, Pallas kernels for 0%

commit v1 on v0

--- a/solution.py
+++ b/solution.py
@@ -48,7 +48,7 @@
         image = jnp.einsum("ijsp,ijsd->dip", u_factors, landed, preferred_element_type=jnp.float32)
         image = image.reshape(dens_count, own_rows * patch_len)
         image_local = jnp.sum(image * image, axis=1)
-        image_sq = lax.psum(image_local, ("row", "col"))
+        image_sq = lax.psum(lax.psum(image_local, "col"), "row")
         step_size = grad_sq / (image_sq + 1e-06)
         densities = densities + step_size[:, None] * grad
         residual = residual - step_size[:, None] * image

time: 596 us -> 500 us (0.84)
  blocking collectives: 221 us -> 129 us
  starting transfers between devices: 20.8 us -> 14.2 us
    psum x2, blocking collectives: 144 us -> 46.7 us  [per_device(): image_sq = lax.psum(lax.psum(image_local, 'col'), 'row')]
    all_to_all x0 -> x1, blocking collectives: none -> 13 us  [per_device(): lax.all_to_all(coefficients, 'col', split_axis=0, concat_axis=1, tiled=True)]
    psum x2, blocking collectives: 66.6 us -> 59.9 us  [per_device(): grad_sq = lax.psum(grad_local, 'col')]
    all_to_all x2 -> x1, starting transfers between devices: 13.1 us -> 6.53 us  [per_device(): lax.all_to_all(coefficients, 'col', split_axis=0, concat_axis=1, tiled=True)]
    all_to_all x2 -> x1, waiting for transfers between devices: 0.01 us -> 6.41 us  [per_device(): lax.all_to_all(coefficients, 'col', split_axis=0, concat_axis=1, tiled=True)]
  transfers between devices with their start and end apart: 6 -> 5, of which waited for: 4 -> 5; matrix products, arithmetic and copies ran while one was open for 0% -> 0% of each run, Pallas kernels for 0% -> 0%
where the time goes in v1:
time: 500 us; the launch traced here: 499 us
  waiting for transfers between devices  270 us (54%)
  blocking collectives  129 us (26%)
  matrix products  52.3 us (10%)
  local copies, waits for them, and re-layouts  14.3 us (3%)
  starting transfers between devices  14.2 us (3%)
  between operations  14 us (3%)
  other arithmetic  5.57 us (1%)
    unnamed x4, waiting for transfers between devices  144 us
    psum x2, waiting for transfers between devices, per_device(): lax.psum(partial_grad.reshape(dens_count, own_cols * patch_len), 'row')  113 us
    psum x2, blocking collectives, per_device(): grad_sq = lax.psum(grad_local, 'col')  59.9 us
    psum x2, blocking collectives, per_device(): image_sq = lax.psum(lax.psum(image_local, 'col'), 'row')  46.7 us
    dot_general x2, matrix products, per_device(): jnp.einsum('ijsp,dip->ijsd', u_factors, res_bf, preferred_element_type=jn...  15.3 us
    all_to_all x1, blocking collectives, per_device(): lax.all_to_all(coefficients, 'col', split_axis=0, concat_axis=1, tiled=True)  13 us
    dot_general x2, matrix products, per_device(): jnp.einsum('ijsp,djp->ijsd', v_factors, grad_bf, preferred_element_type=j...  11.7 us
  transfers between devices with their start and end apart: 5, of which 5 were waited for; matrix products, arithmetic and copies ran while one was open for 0% of the time, Pallas kernels for 0%

profile of v1, /device:TPU:1, one launch (start us, length us, event | category | flops | bytes accessed | tf_op | source)
XLA Modules:
  0.0 498.8 jit_solution(5449829286960815218)
XLA Ops:
  7.2 0.0 copy-start
  7.2 0.0 copy-start.5
  7.2 5.9 %convolution_convert_fusion = bf16[128,48,8]{1,2,0:T(8,128)(2,1)S(1)} fusion(f32[8,512]{1,0:T(8,128)} %param.7, bf16[1,128,48,512]{3,2,1,0:T(8,128)(2,1)} %param.8), kind=kOutput, calls=%fused_computation.14 | convolution fusion | flops 50384896 | bytes 6406144 | tf_op jit(solution)/shard_map/ijsp,dip->ijsd/dot_general | solution.py:24
  13.1 0.2 copy.50
  13.3 0.2 copy.51
  13.5 0.5 broadcast.22
  14.0 1.2 reduce.6
  15.2 0.7 reshape.129
  15.9 7.6 %all-to-all-start = ((bf16[16,2,1536]{2,1,0:T(2,128)(2,1)}), bf16[16,2,1536]{2,1,0:T(2,128)(2,1)S(1)}, u32[]{:S(2)}, u32[]{:S(2)}) async-start(bf16[16,2,1536]{2,1,0:T(2,128)(2,1)} %reshape.129), calls=%async_computation | async-start | bytes 196608 | tf_op jit(solution)/shard_map/all_to_all | solution.py:30
  23.5 0.0 all-reduce.7.cloned.1.call-start
  23.5 0.0 copy-done.5
  23.6 0.1 fusion.38
  23.7 6.6 %all-to-all-done = bf16[16,2,1536]{2,1,0:T(2,128)(2,1)S(1)} async-done(((bf16[16,2,1536]{2,1,0:T(2,128)(2,1)}), bf16[16,2,1536]{2,1,0:T(2,128)(2,1)S(1)}, u32[]{:S(2)}, u32[]{:S(2)}) %all-to-all-start) | async-done | bytes 98336 | tf_op jit(solution)/shard_map/all_to_all | solution.py:30
  30.2 0.1 reshape.130
  30.3 0.6 bitcast_reduce_fusion.1
  30.9 1.8 reshape.105
  32.6 4.8 fusion.8
  37.4 0.0 all-reduce.7.cloned.1.call-update
  37.4 0.0 all-reduce.9.cloned.1.call-start
  37.5 58.1 %all-reduce.7.cloned.1.call-done = f32[8,4096]{1,0:T(8,128)} async-done(((f32[8,4096]{1,0:T(8,128)}), f32[8,4096]{1,0:T(8,128)}) %all-reduce.7.cloned.1.call-update) | async-done | bytes 131088 | tf_op jit(solution)/shard_map/psum | solution.py:35
  95.6 1.1 multiply_reduce_fusion.1
  96.7 5.9 %fusion.22 = bf16[16,8,48,8]{2,3,0,1:T(8,128)(2,1)S(1)} fusion(bf16[8,8,512,1]{2,0,3,1:T(8,128)(2,1)S(1)} %bitcast.89, bf16[16,8,48,512]{3,2,1,0:T(8,128)(2,1)} %param.9, f32[16,8,48]{2,0,1:T(8,128)S(1)} %get-tuple-element.11), kind=kOutput, calls=%fused_computation.15 | convolution fusion | flops 50429952 | bytes 6479872 | tf_op jit(solution)/shard_map/ijsp,djp->ijsd/dot_general | solution.py:40
  102.6 0.5 copy.55
  103.1 0.3 copy.56
  103.4 13.0 %all_to_all.16 = bf16[16,8,384]{2,1,0:T(8,128)(2,1)S(1)} all-to-all(bf16[16,8,384]{2,1,0:T(8,128)(2,1)S(1)} %copy.56), channel_id=1, replica_groups=mesh['row'=8,'col'=16] {'col'}, dimensions={0} | all-to-all | bytes 196608 | tf_op jit(solution)/shard_map/all_to_all | solution.py:46
  116.4 1.8 reshape.109
  118.2 3.8 multiply_reduce_fusion.3
  122.1 29.9 %all-reduce.2 = (f32[8]{0:T(128)S(1)}, f32[8]{0:T(128)S(1)}) all-reduce(f32[8]{0:T(128)S(1)} %get-tuple-element.9, f32[8]{0:T(128)S(1)} %get-tuple-element.13), channel_id=1, replica_groups=mesh['row'=8,'col'=16] {'col'}, use_global_device_ids=true, to_apply=%region_2.0 | all-reduce | flops 16 | bytes 128 | tf_op jit(solution)/shard_map/psum | solution.py:37
  152.0 23.4 %psum.59 = f32[8]{0:T(128)S(1)} all-reduce(f32[8]{0:T(128)S(1)} %get-tuple-element.6), channel_id=1, replica_groups=mesh['row'=8,'col'=16] {'row'}, use_global_device_ids=true, to_apply=%region_5.0 | all-reduce | flops 8 | bytes 64 | tf_op jit(solution)/shard_map/psum | solution.py:51
  175.5 0.0 copy-done.4
  175.5 9.4 %fusion.31 = bf16[1,128,384]{1,2,0:T(8,128)(2,1)S(1)} fusion(bf16[128,48,512]{2,1,0:T(8,128)(2,1)} %bitcast.81, f32[8,512]{1,0:T(8,128)S(1)} %copy-done.4, f32[8,512]{1,0:T(8,128)S(1)} %get-tuple-element.14, f32[8]{0:T(128)S(1)} %add_divide_fusion.1), kind=kOutput, calls=%fused_computation.18 | convolution fusion | flops 50393088 | bytes 6422560 | tf_op jit(solution)/shard_map/ijsp,dip->ijsd/dot_general | solution.py:24
  184.9 0.2 copy.59
  185.1 1.2 reduce.7
  186.3 9.2 %all_to_all.17 = bf16[16,2,1536]{2,1,0:T(2,128)(2,1)S(1)} all-to-all(bf16[16,2,1536]{2,1,0:T(2,128)(2,1)S(1)} %reshape.131), channel_id=1, replica_groups=mesh['row'=8,'col'=16] {'col'}, dimensions={0} | all-to-all | bytes 196608 | tf_op jit(solution)/shard_map/all_to_all | solution.py:30
  195.6 0.1 reshape.132
  195.7 0.6 bitcast_reduce_fusion
  196.2 1.8 reshape.111
  198.0 4.8 fusion.6
  202.8 0.0 all-reduce.9.cloned.1.call-update
  202.8 54.5 %all-reduce.9.cloned.1.call-done = f32[8,4096]{1,0:T(8,128)} async-done(((f32[8,4096]{1,0:T(8,128)}), f32[8,4096]{1,0:T(8,128)}) %all-reduce.9.cloned.1.call-update) | async-done | bytes 131088 | tf_op jit(solution)/shard_map/psum | solution.py:35
  257.3 1.1 fusion.51
  258.4 5.9 %fusion.25 = bf16[16,8,48,8]{2,3,0,1:T(8,128)(2,1)S(1)} fusion(bf16[8,8,512,1]{2,0,3,1:T(8,128)(2,1)S(1)} %bitcast.90, bf16[16,8,48,512]{3,2,1,0:T(8,128)(2,1)} %param.9, f32[16,8,48]{2,0,1:T(8,128)S(1)} %get-tuple-element.11), kind=kOutput, calls=%fused_computation.16 | convolution fusion | flops 50429952 | bytes 6479872 | tf_op jit(solution)/shard_map/ijsp,djp->ijsd/dot_general | solution.py:40
  264.2 0.5 copy.62
  264.8 0.9 copy.63
  265.7 6.5 %all-to-all-start.3 = ((bf16[16,8,384]{2,1,0:T(8,128)(2,1)}), bf16[16,8,384]{2,1,0:T(8,128)(2,1)S(1)}, u32[]{:S(2)}, u32[]{:S(2)}) async-start(bf16[16,8,384]{2,1,0:T(8,128)(2,1)} %copy.63), calls=%async_computation.3 | async-start | bytes 196608 | tf_op jit(solution)/shard_map/all_to_all | solution.py:46
  272.2 0.0 all-reduce.11.cloned.1.call-start
  272.3 0.0 copy-done
  272.3 0.2 dynamic-slice_reduce_fusion
  272.5 6.4 %all-to-all-done.3 = bf16[16,8,384]{2,1,0:T(8,128)(2,1)S(1)} async-done(((bf16[16,8,384]{2,1,0:T(8,128)(2,1)}), bf16[16,8,384]{2,1,0:T(8,128)(2,1)S(1)}, u32[]{:S(2)}, u32[]{:S(2)}) %all-to-all-start.3) | async-done | bytes 98336 | tf_op jit(solution)/shard_map/all_to_all | solution.py:46
  278.9 1.8 reshape.115
  280.7 3.8 multiply_reduce_fusion.2
  284.6 0.0 copy-start.6
  284.6 29.9 %all-reduce.1 = (f32[8]{0:T(128)S(1)}, f32[8]{0:T(128)S(1)}) all-reduce(f32[8]{0:T(128)S(1)} %get-tuple-element.8, f32[8]{0:T(128)S(1)} %get-tuple-element.15), channel_id=1, replica_groups=mesh['row'=8,'col'=16] {'col'}, use_global_device_ids=true, to_apply=%region_8.0 | all-reduce | flops 16 | bytes 128 | tf_op jit(solution)/shard_map/psum | solution.py:37
  314.5 23.3 %psum.63 = f32[8]{0:T(128)S(1)} all-reduce(f32[8]{0:T(128)S(1)} %get-tuple-element.4), channel_id=1, replica_groups=mesh['row'=8,'col'=16] {'row'}, use_global_device_ids=true, to_apply=%region_11.0 | all-reduce | flops 8 | bytes 64 | tf_op jit(solution)/shard_map/psum | solution.py:51
  337.8 0.0 copy-done.2
  337.8 0.0 copy-done.3
  337.8 0.1 multiply_add_fusion
  337.9 0.0 copy-start.1
  337.9 5.7 %convolution_bitcast_fusion = f32[1,2,8,512]{3,2,1,0:T(8,128)S(1)} fusion(bf16[2,512,4096]{2,1,0:T(8,128)(2,1)} %param.11, f32[8,4096]{1,0:T(8,128)S(1)} %multiply_add_fusion), kind=kOutput, calls=%fused_computation.19 | convolution fusion | flops 67141632 | bytes 8552448 | tf_op jit(solution)/shard_map/bpn,dn->bdp/dot_general | solution.py:57
  343.6 2.4 fusion.44
  346.0 0.0 all-reduce.11.cloned.1.call-update
  346.1 0.7 multiply_subtract_fusion
  346.7 144.0 %all-reduce.11.cloned.1.call-done = f32[128,4096]{1,0:T(8,128)} async-done(((f32[128,4096]{1,0:T(8,128)}), f32[128,4096]{1,0:T(8,128)}) %all-reduce.11.cloned.1.call-update) | async-done | bytes 2097168
  490.7 1.5 constant_dynamic-slice_fusion
  (10 shorter events, 0.1 us)
Async XLA Ops:
  7.2 265.1 %copy-start = (s32[16,16]{1,0:T(8,128)S(1)}, s32[16,16]{1,0:T(8,128)}, u32[]{:S(2)}) copy-start(s32[16,16]{1,0:T(8,128)} %param.12) | copy-start | bytes 3076
  7.2 16.4 %copy-start.5 = (s32[16,8]{0,1:T(8,128)S(1)}, s32[16,8]{0,1:T(8,128)}, u32[]{:S(2)}) copy-start(s32[16,8]{0,1:T(8,128)} %param.10) | copy-start | bytes 1540
  15.9 14.3 %all-to-all-start = ((bf16[16,2,1536]{2,1,0:T(2,128)(2,1)}), bf16[16,2,1536]{2,1,0:T(2,128)(2,1)S(1)}, u32[]{:S(2)}, u32[]{:S(2)}) async-start(bf16[16,2,1536]{2,1,0:T(2,128)(2,1)} %reshape.129), calls=%async_computation | async-start | bytes 196608 | tf_op jit(solution)/shard_map/all_to_all | solution.py:30
  23.5 72.1 %all-reduce.7.cloned.1.call-start = ((), (), s32[]{:S(2)}) async-start(), calls=%async_computation.4 | async-start | bytes 262144 | tf_op jit(solution)/shard_map/psum | solution.py:35
  37.4 219.8 %all-reduce.9.cloned.1.call-start = ((), (), s32[]{:S(2)}) async-start(), calls=%async_computation.5 | async-start | bytes 262144 | tf_op jit(solution)/shard_map/psum | solution.py:35
  102.6 72.9 %copy-start.4 = (f32[8,512]{1,0:T(8,128)S(1)}, f32[8,512]{1,0:T(8,128)}, u32[]{:S(2)}) copy-start(f32[8,512]{1,0:T(8,128)} %param.7) | copy-start | bytes 49156
  264.2 73.5 %copy-start.2 = (f32[8,4096]{1,0:T(8,128)S(1)}, f32[8,4096]{1,0:T(8,128)}, u32[]{:S(2)}) copy-start(f32[8,4096]{1,0:T(8,128)} %all-reduce.7.cloned.1.call-done) | copy-start | bytes 393220
  264.2 73.5 %copy-start.3 = (f32[8,4096]{1,0:T(8,128)S(1)}, f32[8,4096]{1,0:T(8,128)}, u32[]{:S(2)}) copy-start(f32[8,4096]{1,0:T(8,128)} %all-reduce.9.cloned.1.call-done) | copy-start | bytes 393220
  265.7 13.2 %all-to-all-start.3 = ((bf16[16,8,384]{2,1,0:T(8,128)(2,1)}), bf16[16,8,384]{2,1,0:T(8,128)(2,1)S(1)}, u32[]{:S(2)}, u32[]{:S(2)}) async-start(bf16[16,8,384]{2,1,0:T(8,128)(2,1)} %copy.63), calls=%async_computation.3 | async-start | bytes 196608 | tf_op jit(solution)/shard_map/all_to_all | solution.py:46
  272.2 218.5 %all-reduce.11.cloned.1.call-start = ((), (), s32[]{:S(2)}) async-start(), calls=%async_computation.6 | async-start | bytes 4194304
  284.6 59.1 %copy-start.6 = (s32[128]{0:T(128)S(1)}, s32[128]{0:T(128)}, u32[]{:S(2)}) copy-start(s32[128]{0:T(128)} %param.13) | copy-start | bytes 1540
  337.9 8.2 %copy-start.1 = (f32[8,4096]{1,0:T(8,128)}, f32[8,4096]{1,0:T(8,128)S(1)}, u32[]{:S(2)}) copy-start(f32[8,4096]{1,0:T(8,128)S(1)} %multiply_add_fusion) | copy-start | bytes 393220
Sparse Core Ops, SparseCore 0:
  37.6 58.0 all-reduce.6
  202.9 54.2 all-reduce.8
  346.2 144.5 all-reduce.10
